TPU v7x, 32 devices: a whole 2x2x4 slice. The times are simulated.
32 devices in a mesh: video: 4 (over x, core), frame: 8 (over z, y).
Axes of the slice: x: 2, y: 2, z: 4, core: 2. Of those that a mesh axis runs over, the one named last changes fastest.
Arguments:
- frames: bfloat16 [32, 1024, 640], P(('video', 'frame')), parts along dimension 0, may hold values from -6 to 6
- ref_rows: bfloat16 [4096, 640], P(('video', 'frame')), parts along dimension 0, may hold values from -6 to 6
- w_query: bfloat16 [640, 640], replicated, may hold values from -1 to 1
- w_key: bfloat16 [640, 640], replicated, may hold values from -1 to 1
- w_value: bfloat16 [640, 640], replicated, may hold values from -0.25 to 0.25
- w_out: bfloat16 [640, 640], replicated, may hold values from -0.25 to 0.25
- w_conv: bfloat16 [3, 640, 640], replicated, may hold values from -0.125 to 0.125
- t_query: bfloat16 [640, 640], replicated, may hold values from -1 to 1
- t_key: bfloat16 [640, 640], replicated, may hold values from -1 to 1
- t_value: bfloat16 [640, 640], replicated, may hold values from -0.25 to 0.25
- t_out: bfloat16 [640, 640], replicated, may hold values from -0.25 to 0.25
Outputs:
- result: bfloat16 [32, 1024, 640], P(('video', 'frame')), parts along dimension 0
There are 4 independent parts, one for each index of `video`. A program takes and returns all parts, laid end to end along the dimension named above; an argument that names none is the same for every part. Nothing has to cross between parts.
All inputs are finite; a program needn't handle non-finite values.
Results may differ from a plain program's by a relative error of at most 0.011.
Values may be sent and summed in bfloat16 or wider, within the bound.
A program may use at most 128 MiB of HBM per device.

v0:
```python
import math

import jax
import jax.numpy as jnp
from jax import lax
from jax.sharding import PartitionSpec as P

HEADS = 10


def padded_2(value, sides, width):
    for axis, dim in sides:
        devices, length = (lax.axis_size(axis), value.shape[dim])
        up = [(i, (i + 1) % devices) for i in range(devices - 1)]
        down = [(j, i) for i, j in up]
        last = lax.slice_in_dim(value, length - width, length, axis=dim)
        leading = lax.slice_in_dim(value, 0, width, axis=dim)
        before = lax.ppermute(last, axis, up)
        after = lax.ppermute(leading, axis, down)
        value = jnp.concatenate([before, value, after], axis=dim)
    return value


def layer_norm(value):
    mean = jnp.mean(value, axis=-1, keepdims=True)
    centered = value - mean
    var = jnp.mean(centered * centered, axis=-1, keepdims=True)
    return centered * lax.rsqrt(var + 1e-05)


def project(rows, weight):
    return jnp.dot(rows, weight, preferred_element_type=jnp.float32).astype(jnp.bfloat16)


def split_heads(value, heads):
    nframes, pixels, width = value.shape
    return value.reshape(nframes, pixels, heads, width // heads).transpose(2, 0, 1, 3)


def temporal_attend(tquery, tkeys, tvalues):
    nframes, pixels, width = tquery.shape
    head_dim = width // HEADS
    shaped_q = tquery.reshape(nframes, pixels, HEADS, head_dim)
    shaped_k = tkeys.reshape(nframes, pixels, HEADS, head_dim)
    shaped_v = tvalues.reshape(nframes, pixels, HEADS, head_dim)
    tscores = jnp.einsum(
        "fnhd,gnhd->nhfg", shaped_q, shaped_k, preferred_element_type=jnp.float32
    ) / math.sqrt(head_dim)
    tpeak = jnp.max(tscores, axis=-1, keepdims=True)
    texpo = jnp.exp(tscores - tpeak)
    ttotal = jnp.sum(texpo, axis=-1)
    tmixed = (
        jnp.einsum(
            "nhfg,gnhd->nhfd",
            texpo.astype(jnp.bfloat16),
            shaped_v,
            preferred_element_type=jnp.float32,
        )
        / ttotal[..., None]
    )
    return tmixed.transpose(2, 0, 1, 3).reshape(nframes, pixels, width).astype(jnp.bfloat16)


def per_device(
    frames, ref_rows, w_query, w_key, w_value, w_out, w_conv, t_query, t_key, t_value, t_out
):
    fdev, pixels, width = frames.shape
    head_dim = width // HEADS
    scale = 1.0 / math.sqrt(head_dim)
    ndev = lax.axis_size("frame")
    group_px = pixels // ndev
    normed = layer_norm(frames.astype(jnp.float32)).astype(jnp.bfloat16).reshape(-1, width)
    query = split_heads(project(normed, w_query).reshape(fdev, pixels, width), HEADS)
    keys = split_heads(project(normed, w_key).reshape(fdev, pixels, width), HEADS)
    values = split_heads(project(normed, w_value).reshape(fdev, pixels, width), HEADS)

    def local_part(args):
        qa, ka, va = args
        scores = jnp.einsum("fqd,fkd->fqk", qa, ka, preferred_element_type=jnp.float32) * scale
        peak = jnp.max(scores, axis=-1)
        expo = jnp.exp(scores - peak[..., None])
        total = jnp.sum(expo, axis=-1)
        accum = jnp.einsum(
            "fqk,fkd->fqd", expo.astype(jnp.bfloat16), va, preferred_element_type=jnp.float32
        )
        return (peak, total, accum)

    start_carry = lax.map(local_part, (query, keys, values))
    ref_keys = project(ref_rows, w_key)
    ref_values = project(ref_rows, w_value)
    piece_keys = lax.all_gather(ref_keys, "frame", axis=0, tiled=True)
    piece_values = lax.all_gather(ref_values, "frame", axis=0, tiled=True)
    count = piece_keys.shape[0]
    heads_k = piece_keys.reshape(count, HEADS, head_dim).transpose(1, 0, 2)
    heads_v = piece_values.reshape(count, HEADS, head_dim).transpose(1, 0, 2)

    def one_head(args):
        qa, peak, total, accum, ka, va = args
        scores = jnp.einsum("fqd,kd->fqk", qa, ka, preferred_element_type=jnp.float32) * scale
        newpeak = jnp.maximum(peak, jnp.max(scores, axis=-1))
        factor = jnp.exp(peak - newpeak)
        expo = jnp.exp(scores - newpeak[..., None])
        total = total * factor + jnp.sum(expo, axis=-1)
        accum = accum * factor[..., None] + jnp.einsum(
            "fqk,kd->fqd", expo.astype(jnp.bfloat16), va, preferred_element_type=jnp.float32
        )
        return (newpeak, total, accum)

    final = lax.map(
        one_head, (query, start_carry[0], start_carry[1], start_carry[2], heads_k, heads_v)
    )
    attended = (
        (final[2] / final[1][..., None])
        .transpose(1, 2, 0, 3)
        .reshape(-1, width)
        .astype(jnp.bfloat16)
    )
    first = (
        frames.astype(jnp.float32)
        + jnp.dot(attended, w_out, preferred_element_type=jnp.float32).reshape(fdev, pixels, width)
    ).astype(jnp.bfloat16)
    padded = padded_2(first, (("frame", 0),), 1)
    conv = jnp.zeros((fdev * pixels, width), jnp.float32)
    for tap in range(3):
        conv = conv + jnp.dot(
            padded[tap : tap + fdev].reshape(-1, width),
            w_conv[tap],
            preferred_element_type=jnp.float32,
        )
    second = (first.astype(jnp.float32) + conv.reshape(fdev, pixels, width)).astype(jnp.bfloat16)
    normed2 = layer_norm(second.astype(jnp.float32)).astype(jnp.bfloat16)
    grouped = normed2.reshape(fdev, ndev, group_px, width)
    features = lax.all_to_all(grouped, "frame", split_axis=1, concat_axis=0, tiled=True)
    nframes, groups, count, channels = features.shape
    flat = features.reshape(-1, channels)
    tquery = project(flat, t_query).reshape(nframes, groups * count, channels)
    tkeys = project(flat, t_key).reshape(nframes, groups * count, channels)
    tvalues = project(flat, t_value).reshape(nframes, groups * count, channels)
    mixed = temporal_attend(tquery, tkeys, tvalues).reshape(nframes, groups, count, channels)
    back = lax.all_to_all(mixed, "frame", split_axis=0, concat_axis=1, tiled=True)
    result = second.astype(jnp.float32) + jnp.dot(
        back.reshape(-1, width), t_out, preferred_element_type=jnp.float32
    ).reshape(fdev, pixels, width)
    return result.astype(jnp.bfloat16)


def solution(mesh):
    return jax.shard_map(
        per_device,
        mesh=mesh,
        in_specs=(
            P(("video", "frame"), None, None),
            P(("video", "frame"), None),
            P(),
            P(),
            P(),
            P(),
            P(),
            P(),
            P(),
            P(),
            P(),
        ),
        out_specs=P(("video", "frame"), None, None),
        check_vma=False,
    )
```

profile of v0, /device:TPU:0, one launch (start us, length us, event | category | flops | bytes accessed | tf_op | source)
XLA Modules:
  0.0 356.5 jit_solution(769306988038147561)
XLA Ops:
  12.7 2.6 convolution_convert_fusion.4
  15.3 2.6 convolution_convert_fusion.3
  20.4 3.3 copy.52
  23.7 3.8 %copy.53 = bf16[1,1024,10,64]{3,1,0,2:T(8,128)(2,1)} copy(bf16[1,1024,10,64]{1,3,2,0:T(8,128)(2,1)} %bitcast.198) | data formatting | bytes 2621440 | tf_op jit(solution)/shard_map/reshape;reshape | solution.py:37
  27.5 3.8 %copy.54 = bf16[1,1024,10,64]{3,1,0,2:T(8,128)(2,1)} copy(bf16[1,1024,10,64]{1,3,2,0:T(8,128)(2,1)} %bitcast.197) | data formatting | bytes 2621440 | tf_op jit(solution)/shard_map/reshape;reshape | solution.py:37
  33.1 49.6 %while.26 = (s32[]{:T(128)}, f32[10,1,1024]{2,1,0:T(1,128)S(1)}, f32[10,1,1024]{2,1,0:T(1,128)S(1)}, f32[10,1,1024,64]{2,3,1,0:T(8,128)}, bf16[10,1,1024,64]{3,2...) while((s32[]{:T(128)}, f32[10,1,1024]{2,1,0:T(1,128)S(1)}, ...), condition=%wide.region_5.6_spmd, body=%wide.region_2.5_spmd.sunk | while | flops 276822016 | bytes 13666393 | solution.py:88
  40.5 2.6 fusion.115
  50.5 2.5 fusion.115
  65.4 2.5 fusion.115
  70.3 2.6 fusion.115
  85.2 11.9 %all-gather.5.cloned.1.call-done = bf16[1024,640]{1,0:T(8,128)(2,1)} async-done(((bf16[128,640]{1,0:T(8,128)(2,1)}), bf16[1024,640]{1,0:T(8,128)(2,1)}) %all-gather.5.cloned.1.call-update) | async-done | bytes 1310736 | tf_op jit(solution)/shard_map/all_gather | solution.py:92
  101.4 51.8 %while.27 = (s32[]{:T(128)}, f32[10,1,1024]{2,0,1:T(8,128)S(1)}, f32[10,1,1024,64]{2,3,1,0:T(8,128)}, f32[10,1,1024]{2,1,0:T(1,128)S(1)}, f32[10,1,1024]{2,1,0:T...) while((s32[]{:T(128)}, f32[10,1,1024]{2,0,1:T(8,128)S(1)}, ...), condition=%wide.region_9.10_spmd, body=%wide.region_6.9_spmd.sunk | while | flops 276959232 | bytes 13707385 | solution.py:109
  103.1 2.6 fusion.119
  108.3 2.6 fusion.119
  113.4 2.6 fusion.119
  118.6 2.6 fusion.119
  123.8 2.6 fusion.119
  129.0 2.6 fusion.119
  134.2 2.6 fusion.119
  139.3 2.6 fusion.119
  144.5 2.6 fusion.119
  149.7 2.6 fusion.119
  162.4 51.6 %collective-permute-done = bf16[1,1024,640]{2,1,0:T(8,128)(2,1)S(1)} collective-permute-done((bf16[1,1024,640]{2,1,0:T(8,128)(2,1)S(1)}, bf16[1,1024,640]{2,1,0:T(8,128)(2,1)S(1)}, u32[]{:S(2)}, u32[]{:S(2)}) %collective-permute-start) | collective-permute-done | bytes 1310752 | tf_op jit(solution)/shard_map/ppermute | solution.py:18
  217.8 36.6 %all_to_all.8 = bf16[1,8,128,640]{3,2,0,1:T(8,128)(2,1)S(1)} all-to-all(bf16[1,8,128,640]{3,2,0,1:T(8,128)(2,1)S(1)} %bitcast.181), channel_id=1, replica_groups=mesh['video'=4,'frame'=8] {'frame'}, dimensions={1} | all-to-all | bytes 2621440 | tf_op jit(solution)/shard_map/all_to_all | solution.py:133
  261.0 7.1 %copy.62 = bf16[8,128,10,64]{3,0,2,1:T(8,128)(2,1)} copy(bf16[8,128,10,64]{1,0,3,2:T(8,128)(2,1)} %bitcast.185) | data formatting | bytes 2621440 | tf_op jit(solution)/shard_map/reshape;reshape | solution.py:43
  273.5 7.1 %copy.63 = bf16[8,128,10,64]{3,0,2,1:T(8,128)(2,1)} copy(bf16[8,128,10,64]{1,0,3,2:T(8,128)(2,1)} %bitcast.186) | data formatting | bytes 2621440 | tf_op jit(solution)/shard_map/reshape;reshape | solution.py:44
  286.0 7.2 %copy.66 = bf16[8,128,10,64]{3,0,2,1:T(8,128)(2,1)} copy(bf16[8,128,10,64]{1,0,3,2:T(8,128)(2,1)} %bitcast.187) | data formatting | bytes 2621440 | tf_op jit(solution)/shard_map/reshape;reshape | solution.py:45
  293.2 4.6 %multiply_reduce_fusion.2 = (f32[128,10,8]{2,1,0:T(8,128)S(1)}, f32[128,10,8,8]{2,3,1,0:T(8,128)S(1)}) fusion(bf16[8,128,10,64]{3,0,2,1:T(8,128)(2,1)} %copy.62, bf16[8,128,10,64]{3,0,2,1:T(8,128)(2,1)} %copy.63), kind=kOutput, calls=%fused_computation.47 | convolution fusion | flops 10639360 | bytes 2990080 | tf_op jit(solution)/shard_map/fnhd,gnhd->nhfg/dot_general | solution.py:46
  300.1 3.9 %fusion.45 = bf16[8,128,10,64]{3,0,2,1:T(8,128)(2,1)} fusion(f32[8,128,10]{0,2,1:T(8,128)S(1)} %bitcast.200, bf16[8,128,10,64]{3,0,2,1:T(8,128)(2,1)S(1)} %copy-done.4, f32[128,10,8,8]{2,3,1,0:T(8,128)S(1)} %get-tuple-element.167, f32[128,10,8]{2,1,0:T(8,128)S(1)} %get-tuple-element.166), kind=kOutput, calls=%fused_computation.45 | convolution fusion | flops 12042240 | bytes 3031040 | tf_op jit(solution)/shard_map/nhfg,gnhd->nhfd/dot_general | solution.py:53
  304.0 5.1 %copy.67 = bf16[8,128,10,64]{1,3,2,0:T(8,128)(2,1)} copy(bf16[8,128,10,64]{3,0,2,1:T(8,128)(2,1)} %fusion.45) | data formatting | bytes 2621440 | tf_op jit(solution)/shard_map/convert_element_type | solution.py:61
  309.1 34.7 %all_to_all.9 = bf16[8,1,128,640]{2,3,1,0:T(8,128)(2,1)S(1)} all-to-all(bf16[8,1,128,640]{2,3,1,0:T(8,128)(2,1)} %bitcast.188), channel_id=1, replica_groups=mesh['video'=4,'frame'=8] {'frame'}, dimensions={0} | all-to-all | bytes 2621440 | tf_op jit(solution)/shard_map/all_to_all | solution.py:140
  345.2 4.0 %fusion.57 = bf16[1,1024,640]{2,1,0:T(8,128)(2,1)} fusion(bf16[1,1024,640]{2,1,0:T(8,128)(2,1)S(1)} %get-tuple-element.165, bf16[1024,640]{1,0:T(8,128)(2,1)} %bitcast.196, bf16[640,640]{1,0:T(8,128)(2,1)} %param.25), kind=kOutput, calls=%fused_computation.65 | convolution fusion | flops 840826880 | bytes 4751360 | tf_op jit(solution)/shard_map/dot_general | solution.py:141
  (168 shorter events, 116.0 us)
Async XLA Ops:
  6.5 1.1 copy-start
  6.5 5.4 %copy-start.2 = (bf16[1,1024,640]{2,1,0:T(8,128)(2,1)S(1)}, bf16[1,1024,640]{2,1,0:T(8,128)(2,1)}, u32[]{:S(2)}) copy-start(bf16[1,1024,640]{2,1,0:T(8,128)(2,1)} %param.15) | copy-start | bytes 3932164
  6.5 76.2 %all-gather.3.cloned.1.call-start = ((), (), s32[]{:S(2)}) async-start(), calls=%async_computation.2 | async-start | bytes 1474560 | tf_op jit(solution)/shard_map/all_gather | solution.py:91
  9.6 87.5 %all-gather.5.cloned.1.call-start = ((), (), s32[]{:S(2)}) async-start(), calls=%async_computation.3 | async-start | bytes 1474560 | tf_op jit(solution)/shard_map/all_gather | solution.py:92
  12.7 2.6 copy-start.8
  15.3 2.6 copy-start.10
  153.2 2.3 copy-start.3
  153.2 2.3 copy-start.11
  155.5 5.5 %copy-start.9 = (bf16[3,640,640]{2,1,0:T(8,128)(2,1)S(1)}, bf16[3,640,640]{2,1,0:T(8,128)(2,1)}, u32[]{:S(2)}) copy-start(bf16[3,640,640]{2,1,0:T(8,128)(2,1)} %param.21) | copy-start | bytes 7372804
  157.0 57.0 %collective-permute-start = (bf16[1,1024,640]{2,1,0:T(8,128)(2,1)S(1)}, bf16[1,1024,640]{2,1,0:T(8,128)(2,1)S(1)}, u32[]{:S(2)}, u32[]{:S(2)}) collective-permute-start(bf16[1,1024,640]{2,1,0:T(8,128)(2,1)S(1)} %fusion.56), channel_id=1, source_target_pairs={{0,1},{1,2},{2,3},{3,4},{4,5},{5,6},{6,7},{8,9},{9,10},{10,11},{11... | collective-permute-start | bytes 3932168 | tf_op jit(solution)/shard_map/ppermute | solution.py:18
  159.5 55.8 %collective-permute-start.1 = (bf16[1,1024,640]{2,1,0:T(8,128)(2,1)S(1)}, bf16[1,1024,640]{2,1,0:T(8,128)(2,1)S(1)}, u32[]{:S(2)}, u32[]{:S(2)}) collective-permute-start(bf16[1,1024,640]{2,1,0:T(8,128)(2,1)S(1)} %fusion.56), channel_id=1, source_target_pairs={{1,0},{2,1},{3,2},{4,3},{5,4},{6,5},{7,6},{9,8},{10,9},{11,10},{12... | collective-permute-start | bytes 3932168 | tf_op jit(solution)/shard_map/ppermute | solution.py:19
  217.4 38.2 %copy-start.12 = (bf16[640,640]{1,0:T(8,128)(2,1)S(1)}, bf16[640,640]{1,0:T(8,128)(2,1)}, u32[]{:S(2)}) copy-start(bf16[640,640]{1,0:T(8,128)(2,1)} %param.22) | copy-start | bytes 2457604
  254.4 1.1 copy-start.5
  261.0 7.1 %copy-start.6 = (bf16[1,8,128,640]{3,2,0,1:T(8,128)(2,1)S(1)}, bf16[1,8,128,640]{3,2,0,1:T(8,128)(2,1)}, u32[]{:S(2)}) copy-start(bf16[1,8,128,640]{3,2,0,1:T(8,128)(2,1)} %copy-done.5) | copy-start | bytes 3932164
  261.0 7.1 %copy-start.13 = (bf16[640,640]{1,0:T(8,128)(2,1)S(1)}, bf16[640,640]{1,0:T(8,128)(2,1)}, u32[]{:S(2)}) copy-start(bf16[640,640]{1,0:T(8,128)(2,1)} %param.23) | copy-start | bytes 2457604
  273.5 7.1 %copy-start.7 = (bf16[1,8,128,640]{3,2,0,1:T(8,128)(2,1)S(1)}, bf16[1,8,128,640]{3,2,0,1:T(8,128)(2,1)}, u32[]{:S(2)}) copy-start(bf16[1,8,128,640]{3,2,0,1:T(8,128)(2,1)} %copy-done.5) | copy-start | bytes 3932164
  273.5 7.1 %copy-start.14 = (bf16[640,640]{1,0:T(8,128)(2,1)S(1)}, bf16[640,640]{1,0:T(8,128)(2,1)}, u32[]{:S(2)}) copy-start(bf16[640,640]{1,0:T(8,128)(2,1)} %param.24) | copy-start | bytes 2457604
  297.8 2.2 copy-start.4
  345.2 4.0 %copy-start.1 = (bf16[640,640]{1,0:T(8,128)(2,1)S(1)}, bf16[640,640]{1,0:T(8,128)(2,1)}, u32[]{:S(2)}) copy-start(bf16[640,640]{1,0:T(8,128)(2,1)} %param.18) | copy-start | bytes 2457604
Sparse Core Ops, SparseCore 0:
  9.7 44.5 all-gather.2
  56.5 40.5 all-gather.4
where the time goes:
time: 362 us; the launch traced here: 356 us
  matrix products  122 us (34%)
  blocking collectives  71.3 us (20%)
  waiting for transfers between devices  63.5 us (18%)
  local copies, waits for them, and re-layouts  60.2 us (17%)
  other arithmetic  21.1 us (6%)
  between operations  14.1 us (4%)
  starting transfers between devices  4.08 us (1%)
    ppermute x1, waiting for transfers between devices, padded_2(): before = lax.ppermute(last, axis, up)  51.6 us
    all_to_all x1, blocking collectives, per_device(): lax.all_to_all(grouped, 'frame', split_axis=1, concat_axis=0, tiled=True)  36.6 us
    all_to_all x1, blocking collectives, per_device(): lax.all_to_all(mixed, 'frame', split_axis=0, concat_axis=1, tiled=True)  34.7 us
    dot_general x10, matrix products, one_head(): jnp.einsum('fqk,kd->fqd', expo.astype(jnp.bfloat16), va, preferred_elemen...  25.7 us
    dot_general x10, matrix products, local_part(): jnp.einsum('fqk,fkd->fqd', expo.astype(jnp.bfloat16), va, preferred_eleme...  25.4 us
    dot_general x8, matrix products, project(): jnp.dot(rows, weight, preferred_element_type=jnp.float32)  18.9 us
    dot_general x10, matrix products, one_head(): jnp.einsum('fqd,kd->fqk', qa, ka, preferred_element_type=jnp.float32)  16.7 us
    dot_general x10, matrix products, local_part(): jnp.einsum('fqd,fkd->fqk', qa, ka, preferred_element_type=jnp.float32)  16.7 us
  transfers between devices with their start and end apart: 4, of which 2 were waited for; matrix products, arithmetic and copies ran while one was open for 22% of the time, Pallas kernels for 0%

commit v1 on v0

v1 whole, which is shorter than its diff:
```python
import functools
import math

import jax
import jax.numpy as jnp
from jax import lax
from jax.experimental import pallas as pl
from jax.experimental.pallas import tpu as pltpu
from jax.sharding import PartitionSpec as P

HEADS = 10
F32 = jnp.float32
BF16 = jnp.bfloat16
LOG2E = math.log2(math.e)
CHUNKS = 2


def layer_norm(value):
    mean = jnp.mean(value, axis=-1, keepdims=True)
    centered = value - mean
    var = jnp.mean(centered * centered, axis=-1, keepdims=True)
    return centered * lax.rsqrt(var + 1e-05)


def dot(a, b):
    return jnp.dot(a, b, preferred_element_type=F32)


def dot_nt(a, b):
    return lax.dot_general(a, b, (((1,), (1,)), ((), ())), preferred_element_type=F32)


def remote(src, dst, send, recv, device):
    return pltpu.make_async_remote_copy(
        src_ref=src,
        dst_ref=dst,
        send_sem=send,
        recv_sem=recv,
        device_id={"frame": device},
        device_id_type=pl.DeviceIdType.MESH,
    )


def kernel(
    ndev,
    x_ref,
    own_ref,
    wq,
    wk,
    wv,
    wo,
    wc,
    tq,
    tk,
    tv,
    to,
    out_ref,
    refbuf,
    qbuf,
    kbuf,
    vbuf,
    abuf,
    fbuf,
    rbuf,
    sbuf,
    tqb,
    tkb,
    tvb,
    tab,
    resbuf,
    ref_send,
    ref_recv,
    fwd_send,
    there_send,
    there_recv,
    back_send,
    back_recv,
    local_sem,
):
    pixels, width = x_ref.shape
    pairs = HEADS // 2
    head_dim = width // HEADS
    qscale = LOG2E / math.sqrt(head_dim)
    group = pixels // ndev
    block = 2 * group
    nblocks = pixels // block
    me = lax.axis_index("frame")
    partner = me + 1 - 2 * lax.rem(me, 2)
    line = me // 2

    barrier = pltpu.get_barrier_semaphore()
    for off in range(1, ndev):
        pl.semaphore_signal(
            barrier,
            inc=1,
            device_id={"frame": lax.rem(me + off, ndev)},
            device_id_type=pl.DeviceIdType.MESH,
        )
    pl.semaphore_wait(barrier, ndev - 1)

    def ref_copy(target, slot):
        return remote(own_ref, refbuf.at[me], ref_send.at[slot], ref_recv.at[me], target)

    def ref_forward(owner, slot):
        return remote(
            refbuf.at[owner], refbuf.at[owner], fwd_send.at[slot], ref_recv.at[owner], partner
        )

    hops = ndev // 2
    for hop in range(1, hops):
        ref_copy(lax.rem(me + 2 * hop, ndev), hop).start()
    ref_copy(partner, 0).start()

    def own_rows(step, carry):
        rows = pl.ds(pl.multiple_of(step * block, block), block)
        normed = layer_norm(x_ref[rows, :].astype(F32)).astype(BF16)
        qbuf[rows, :] = (dot(normed, wq[...]) * qscale).astype(BF16)
        kbuf[rows, :] = dot(normed, wk[...]).astype(BF16)
        values = dot(normed, wv[...]).astype(BF16)
        for pair in range(pairs):
            vbuf[pair, rows, 0:128] = values[:, pair * 128 : pair * 128 + 128]
            vbuf[pair, rows, 128:256] = jnp.ones((block, 128), BF16)
        return carry

    lax.fori_loop(0, nblocks, own_rows, 0)

    for hop in range(1, hops):
        owner = lax.rem(me + 2 * hop, ndev)
        ref_forward(owner, hop).wait_recv()
        ref_forward(owner, hop).start()

    def ref_project(rows_in, owner):
        rows = pl.ds(pl.multiple_of(pixels + owner * group, group), group)
        kbuf[rows, :] = dot(rows_in, wk[...]).astype(BF16)
        values = dot(rows_in, wv[...]).astype(BF16)
        for pair in range(pairs):
            vbuf[pair, rows, 0:128] = values[:, pair * 128 : pair * 128 + 128]
            vbuf[pair, rows, 128:256] = jnp.ones((group, 128), BF16)

    ref_project(own_ref[...], me)

    def line_rows(hop, carry):
        owner = lax.rem(me + 2 * hop, ndev)
        ref_project(refbuf[owner], owner)
        return carry

    lax.fori_loop(1, hops, line_rows, 0)

    def partner_rows(hop, carry):
        owner = lax.rem(partner + 2 * hop, ndev)
        ref_forward(owner, 0).wait_recv()
        ref_project(refbuf[owner], owner)
        return carry

    lax.fori_loop(0, hops, partner_rows, 0)

    low = lax.broadcasted_iota(jnp.int32, (block, 128), 1) < 64

    def send_there(target):
        return remote(
            fbuf.at[target], rbuf.at[me], there_send.at[target], there_recv.at[me], target
        )

    def attend(step, carry):
        back = nblocks - 1 - step
        where_to = lax.rem(line + lax.rem((back * (back + 1)) // 2, nblocks), nblocks)
        rows = pl.ds(pl.multiple_of(where_to * block, block), block)

        def one_pair(pair, carry):
            lanes = pl.ds(pl.multiple_of(pair * 128, 128), 128)
            queries = qbuf[rows, lanes]
            keys = kbuf[:, lanes]
            values = vbuf[pair]
            mixed = []
            for half in range(2):
                zero = jnp.zeros_like(queries)
                masked = jnp.where(low, queries, zero) if half == 0 else jnp.where(low, zero, queries)
                scores = dot_nt(masked, keys)
                peak = jnp.max(scores, axis=-1, keepdims=True)
                expo = jnp.exp2(scores - peak).astype(BF16)
                both = dot(expo, values)
                mixed.append(both[:, :128] / both[:, 128:])
            abuf[:, lanes] = jnp.where(low, mixed[0], mixed[1]).astype(BF16)
            return carry

        lax.fori_loop(0, pairs, one_pair, 0)
        first = (x_ref[rows, :].astype(F32) + dot(abuf[...], wo[...])).astype(BF16)
        for half in range(2):
            target = 2 * where_to + half
            fbuf[target] = first[half * group : (half + 1) * group]

            @pl.when(target != me)
            def _():
                send_there(target).start()

        return carry

    lax.fori_loop(0, nblocks, attend, 0)

    keep = pltpu.make_async_copy(fbuf.at[me], rbuf.at[me], local_sem)
    keep.start()
    keep.wait()
    for off in range(1, ndev):
        other = lax.rem(me + off, ndev)
        remote(
            fbuf.at[other], rbuf.at[other], there_send.at[other], there_recv.at[other], other
        ).wait()

    size = group // CHUNKS
    span = ndev * 16
    tlow = lax.broadcasted_iota(jnp.int32, (span, 128), 1) < 64
    same = lax.rem(lax.broadcasted_iota(jnp.int32, (span, span), 0), 16) == lax.rem(
        lax.broadcasted_iota(jnp.int32, (span, span), 1), 16
    )

    def back_copy(chunk, target, sender):
        return remote(
            resbuf.at[chunk, target],
            out_ref.at[pl.ds(pl.multiple_of(sender * group + chunk * size, size), size)],
            back_send.at[chunk * ndev + target],
            back_recv.at[chunk * ndev + sender],
            target,
        )

    def temporal(chunk, carry):
        cols = pl.ds(pl.multiple_of(chunk * size, size), size)
        x = rbuf[:, cols, :].reshape(ndev * size, width)
        edge = jnp.zeros((size, width), BF16)
        before = jnp.concatenate([edge, x[:-size]], axis=0)
        after = jnp.concatenate([x[size:], edge], axis=0)
        conv = dot(before, wc[0]) + dot(x, wc[1]) + dot(after, wc[2])
        second = (x.astype(F32) + conv).astype(BF16)
        sbuf[...] = second
        normed = layer_norm(second.astype(F32)).astype(BF16)
        tqb[...] = (dot(normed, tq[...]) * qscale).astype(BF16).reshape(ndev, size, width)
        tkb[...] = dot(normed, tk[...]).astype(BF16).reshape(ndev, size, width)
        tvb[...] = dot(normed, tv[...]).astype(BF16).reshape(ndev, size, width)

        def sub(index, carry):
            part = pl.ds(pl.multiple_of(index * 16, 16), 16)
            for pair in range(pairs):
                lanes = pl.ds(pair * 128, 128)
                queries = tqb[:, part, lanes].reshape(span, 128)
                keys = tkb[:, part, lanes].reshape(span, 128)
                values = tvb[:, part, lanes].reshape(span, 128)
                zero = jnp.zeros_like(queries)
                mixed = []
                for half in range(2):
                    masked = (
                        jnp.where(tlow, queries, zero) if half == 0 else jnp.where(tlow, zero, queries)
                    )
                    scores = jnp.where(same, dot_nt(masked, keys), -1e30)
                    peak = jnp.max(scores, axis=-1, keepdims=True)
                    expo = jnp.exp2(scores - peak)
                    total = jnp.sum(expo, axis=-1, keepdims=True)
                    mixed.append(dot(expo.astype(BF16), values) / total)
                tab[:, part, lanes] = (
                    jnp.where(tlow, mixed[0], mixed[1]).astype(BF16).reshape(ndev, 16, 128)
                )
            return carry

        lax.fori_loop(0, size // 16, sub, 0)
        result = sbuf[...].astype(F32) + dot(tab[...].reshape(ndev * size, width), to[...])
        resbuf[chunk] = result.astype(BF16).reshape(ndev, size, width)
        for off in range(1, ndev):
            back_copy(chunk, lax.rem(me + off, ndev), me).start()
        out_ref[pl.ds(pl.multiple_of(me * group + chunk * size, size), size), :] = resbuf[chunk, me]
        return carry

    lax.fori_loop(0, CHUNKS, temporal, 0)

    ref_copy(partner, 0).wait_send()
    for hop in range(1, hops):
        owner = lax.rem(me + 2 * hop, ndev)
        ref_copy(owner, hop).wait_send()
        ref_forward(owner, hop).wait_send()
    for chunk in range(CHUNKS):
        for off in range(1, ndev):
            other = lax.rem(me + off, ndev)
            back_copy(chunk, other, me).wait_send()
            back_copy(chunk, other, other).wait_recv()


def per_device(
    frames, ref_rows, w_query, w_key, w_value, w_out, w_conv, t_query, t_key, t_value, t_out
):
    fdev, pixels, width = frames.shape
    ndev = lax.axis_size("frame")
    group = pixels // ndev
    block = 2 * group
    pairs = HEADS // 2
    size = group // CHUNKS
    DMA = pltpu.SemaphoreType.DMA
    out = pl.pallas_call(
        functools.partial(kernel, ndev),
        out_shape=jax.ShapeDtypeStruct((pixels, width), BF16),
        in_specs=[pl.BlockSpec(memory_space=pltpu.VMEM)] * 11,
        out_specs=pl.BlockSpec(memory_space=pltpu.VMEM),
        scratch_shapes=[
            pltpu.VMEM((ndev, group, width), BF16),
            pltpu.VMEM((pixels, width), BF16),
            pltpu.VMEM((2 * pixels, width), BF16),
            pltpu.VMEM((pairs, 2 * pixels, 256), BF16),
            pltpu.VMEM((block, width), BF16),
            pltpu.VMEM((ndev, group, width), BF16),
            pltpu.VMEM((ndev, group, width), BF16),
            pltpu.VMEM((ndev * size, width), BF16),
            pltpu.VMEM((ndev, size, width), BF16),
            pltpu.VMEM((ndev, size, width), BF16),
            pltpu.VMEM((ndev, size, width), BF16),
            pltpu.VMEM((ndev, size, width), BF16),
            pltpu.VMEM((CHUNKS, ndev, size, width), BF16),
            DMA((ndev,)),
            DMA((ndev,)),
            DMA((ndev,)),
            DMA((ndev,)),
            DMA((ndev,)),
            DMA((CHUNKS * ndev,)),
            DMA((CHUNKS * ndev,)),
            DMA(()),
        ],
        compiler_params=pltpu.CompilerParams(
            collective_id=0, has_side_effects=True, vmem_limit_bytes=60 * 1024 * 1024
        ),
    )(
        frames.reshape(pixels, width),
        ref_rows,
        w_query,
        w_key,
        w_value,
        w_out,
        w_conv,
        t_query,
        t_key,
        t_value,
        t_out,
    )
    return out.reshape(fdev, pixels, width)


def solution(mesh):
    return jax.shard_map(
        per_device,
        mesh=mesh,
        in_specs=(
            P(("video", "frame"), None, None),
            P(("video", "frame"), None),
            P(),
            P(),
            P(),
            P(),
            P(),
            P(),
            P(),
            P(),
            P(),
        ),
        out_specs=P(("video", "frame"), None, None),
        check_vma=False,
    )
```

time: 362 us -> 128 us (0.35)
  the two profiles are of different devices: /device:TPU:0 before, /device:TPU:31 now
where the time goes in v1:
time: 128 us
  Pallas kernels  126 us (98%)
  local copies, waits for them, and re-layouts  2.49 us (2%)
    pallas_call x1, Pallas kernels, per_device(): pl.pallas_call(functools.partial(kernel, ndev), out_shape=jax.ShapeDtypeS...  126 us

profile of v1, /device:TPU:31, one launch (start us, length us, event | category | flops | bytes accessed | tf_op | source)
XLA Modules:
  0.0 128.2 jit_solution(17348494194562390388)
XLA Ops:
  0.0 125.7 %shard_map.109 = bf16[1024,640]{1,0:T(8,128)(2,1)} custom-call(bf16[1024,640]{1,0:T(8,128)(2,1)} %bitcast.3, bf16[128,640]{1,0:T(8,128)(2,1)} %own_ref.1, bf16[640,640]{1,0:T(8,128)(2,1)} %wq.1, bf16[640,640]{1,0:T(8,128)(2,1)} %wk.1, bf16[640,640]{1,0:T(8,128)(2,1)} %wv.1, bf16[640,640]{1,0:T(8,128)(2,1)} %wo.1, bf16[3,640,640]{2,1,0:T(8,128)(2,1)} %wc.1, ...), custom_call_target="tpu_custom_call" | custom-call | tf_op jit(solution)/shard_map/pallas_call | solution.py:294
  125.7 2.5 %copy.13 = bf16[1,1024,640]{2,1,0:T(8,128)(2,1)} copy(bf16[1,1024,640]{2,1,0:T(8,128)(2,1)} %bitcast.2) | data formatting | bytes 2621440

commit v2 on v1

--- a/solution.py
+++ b/solution.py
@@ -12,7 +12,7 @@
 F32 = jnp.float32
 BF16 = jnp.bfloat16
 LOG2E = math.log2(math.e)
-CHUNKS = 2
+CHUNKS = 4
 
 
 def layer_norm(value):
@@ -75,18 +75,16 @@
     there_recv,
     back_send,
     back_recv,
-    local_sem,
 ):
-    pixels, width = x_ref.shape
+    group, width = x_ref.shape[1:]
+    pixels = ndev * group
     pairs = HEADS // 2
     head_dim = width // HEADS
     qscale = LOG2E / math.sqrt(head_dim)
-    group = pixels // ndev
-    block = 2 * group
-    nblocks = pixels // block
+    size = group // CHUNKS
+    block = ndev * size
     me = lax.axis_index("frame")
     partner = me + 1 - 2 * lax.rem(me, 2)
-    line = me // 2
 
     barrier = pltpu.get_barrier_semaphore()
     for off in range(1, ndev):
@@ -112,17 +110,20 @@
     ref_copy(partner, 0).start()
 
     def own_rows(step, carry):
-        rows = pl.ds(pl.multiple_of(step * block, block), block)
-        normed = layer_norm(x_ref[rows, :].astype(F32)).astype(BF16)
-        qbuf[rows, :] = (dot(normed, wq[...]) * qscale).astype(BF16)
+        rows = pl.ds(pl.multiple_of(step * 2 * group, 2 * group), 2 * group)
+        both = pl.ds(step * 2, 2)
+        x = x_ref[both].reshape(2 * group, width)
+        normed = layer_norm(x.astype(F32)).astype(BF16)
+        queries = (dot(normed, wq[...]) * qscale).astype(BF16)
+        qbuf[both] = queries.reshape(2, group, width)
         kbuf[rows, :] = dot(normed, wk[...]).astype(BF16)
         values = dot(normed, wv[...]).astype(BF16)
         for pair in range(pairs):
             vbuf[pair, rows, 0:128] = values[:, pair * 128 : pair * 128 + 128]
-            vbuf[pair, rows, 128:256] = jnp.ones((block, 128), BF16)
+            vbuf[pair, rows, 128:256] = jnp.ones((2 * group, 128), BF16)
         return carry
 
-    lax.fori_loop(0, nblocks, own_rows, 0)
+    lax.fori_loop(0, ndev // 2, own_rows, 0)
 
     for hop in range(1, hops):
         owner = lax.rem(me + 2 * hop, ndev)
@@ -156,19 +157,21 @@
 
     low = lax.broadcasted_iota(jnp.int32, (block, 128), 1) < 64
 
-    def send_there(target):
+    def there_copy(chunk, target, sender):
         return remote(
-            fbuf.at[target], rbuf.at[me], there_send.at[target], there_recv.at[me], target
+            fbuf.at[chunk, target],
+            rbuf.at[chunk, sender],
+            there_send.at[chunk * ndev + target],
+            there_recv.at[chunk * ndev + sender],
+            target,
         )
 
-    def attend(step, carry):
-        back = nblocks - 1 - step
-        where_to = lax.rem(line + lax.rem((back * (back + 1)) // 2, nblocks), nblocks)
-        rows = pl.ds(pl.multiple_of(where_to * block, block), block)
-
-        def one_pair(pair, carry):
-            lanes = pl.ds(pl.multiple_of(pair * 128, 128), 128)
-            queries = qbuf[rows, lanes]
+    def attend(chunk):
+        rows = pl.ds(pl.multiple_of(chunk * size, size), size)
+
+        for pair in range(pairs):
+            lanes = pl.ds(pair * 128, 128)
+            queries = qbuf[:, rows, lanes].reshape(block, 128)
             keys = kbuf[:, lanes]
             values = vbuf[pair]
             mixed = []
@@ -181,32 +184,14 @@
                 both = dot(expo, values)
                 mixed.append(both[:, :128] / both[:, 128:])
             abuf[:, lanes] = jnp.where(low, mixed[0], mixed[1]).astype(BF16)
-            return carry
-
-        lax.fori_loop(0, pairs, one_pair, 0)
-        first = (x_ref[rows, :].astype(F32) + dot(abuf[...], wo[...])).astype(BF16)
-        for half in range(2):
-            target = 2 * where_to + half
-            fbuf[target] = first[half * group : (half + 1) * group]
-
-            @pl.when(target != me)
-            def _():
-                send_there(target).start()
-
-        return carry
-
-    lax.fori_loop(0, nblocks, attend, 0)
-
-    keep = pltpu.make_async_copy(fbuf.at[me], rbuf.at[me], local_sem)
-    keep.start()
-    keep.wait()
-    for off in range(1, ndev):
-        other = lax.rem(me + off, ndev)
-        remote(
-            fbuf.at[other], rbuf.at[other], there_send.at[other], there_recv.at[other], other
-        ).wait()
-
-    size = group // CHUNKS
+
+        x = x_ref[:, rows, :].reshape(block, width).astype(F32)
+        first = (x + dot(abuf[...], wo[...])).astype(BF16)
+        fbuf[chunk] = first.reshape(ndev, size, width)
+        for off in reversed(range(1, ndev)):
+            there_copy(chunk, lax.rem(me + off, ndev), me).start()
+        rbuf[chunk, me] = fbuf[chunk, me]
+
     span = ndev * 16
     tlow = lax.broadcasted_iota(jnp.int32, (span, 128), 1) < 64
     same = lax.rem(lax.broadcasted_iota(jnp.int32, (span, span), 0), 16) == lax.rem(
@@ -222,9 +207,10 @@
             target,
         )
 
-    def temporal(chunk, carry):
-        cols = pl.ds(pl.multiple_of(chunk * size, size), size)
-        x = rbuf[:, cols, :].reshape(ndev * size, width)
+    def temporal(chunk):
+        for off in range(1, ndev):
+            there_copy(chunk, lax.rem(me + off, ndev), lax.rem(me + off, ndev)).wait_recv()
+        x = rbuf[chunk].reshape(ndev * size, width)
         edge = jnp.zeros((size, width), BF16)
         before = jnp.concatenate([edge, x[:-size]], axis=0)
         after = jnp.concatenate([x[size:], edge], axis=0)
@@ -265,9 +251,19 @@
         for off in range(1, ndev):
             back_copy(chunk, lax.rem(me + off, ndev), me).start()
         out_ref[pl.ds(pl.multiple_of(me * group + chunk * size, size), size), :] = resbuf[chunk, me]
+
+    def stage(step, carry):
+        @pl.when(step < CHUNKS)
+        def _():
+            attend(step)
+
+        @pl.when(step >= 1)
+        def _():
+            temporal(step - 1)
+
         return carry
 
-    lax.fori_loop(0, CHUNKS, temporal, 0)
+    lax.fori_loop(0, CHUNKS + 1, stage, 0)
 
     ref_copy(partner, 0).wait_send()
     for hop in range(1, hops):
@@ -277,6 +273,7 @@
     for chunk in range(CHUNKS):
         for off in range(1, ndev):
             other = lax.rem(me + off, ndev)
+            there_copy(chunk, other, me).wait_send()
             back_copy(chunk, other, me).wait_send()
             back_copy(chunk, other, other).wait_recv()
 
@@ -287,9 +284,9 @@
     fdev, pixels, width = frames.shape
     ndev = lax.axis_size("frame")
     group = pixels // ndev
-    block = 2 * group
     pairs = HEADS // 2
     size = group // CHUNKS
+    block = ndev * size
     DMA = pltpu.SemaphoreType.DMA
     out = pl.pallas_call(
         functools.partial(kernel, ndev),
@@ -298,13 +295,13 @@
         out_specs=pl.BlockSpec(memory_space=pltpu.VMEM),
         scratch_shapes=[
             pltpu.VMEM((ndev, group, width), BF16),
-            pltpu.VMEM((pixels, width), BF16),
+            pltpu.VMEM((ndev, group, width), BF16),
             pltpu.VMEM((2 * pixels, width), BF16),
             pltpu.VMEM((pairs, 2 * pixels, 256), BF16),
             pltpu.VMEM((block, width), BF16),
-            pltpu.VMEM((ndev, group, width), BF16),
-            pltpu.VMEM((ndev, group, width), BF16),
-            pltpu.VMEM((ndev * size, width), BF16),
+            pltpu.VMEM((CHUNKS, ndev, size, width), BF16),
+            pltpu.VMEM((CHUNKS, ndev, size, width), BF16),
+            pltpu.VMEM((block, width), BF16),
             pltpu.VMEM((ndev, size, width), BF16),
             pltpu.VMEM((ndev, size, width), BF16),
             pltpu.VMEM((ndev, size, width), BF16),
@@ -313,17 +310,16 @@
             DMA((ndev,)),
             DMA((ndev,)),
             DMA((ndev,)),
-            DMA((ndev,)),
-            DMA((ndev,)),
             DMA((CHUNKS * ndev,)),
             DMA((CHUNKS * ndev,)),
-            DMA(()),
+            DMA((CHUNKS * ndev,)),
+            DMA((CHUNKS * ndev,)),
         ],
         compiler_params=pltpu.CompilerParams(
             collective_id=0, has_side_effects=True, vmem_limit_bytes=60 * 1024 * 1024
         ),
     )(
-        frames.reshape(pixels, width),
+        frames.reshape(ndev, group, width),
         ref_rows,
         w_query,
         w_key,

time: 128 us -> 109 us (0.85)
  the two profiles are of different devices: /device:TPU:31 before, /device:TPU:0 now
where the time goes in v2:
time: 109 us; the launch traced here: 108 us
  Pallas kernels  106 us (97%)
  local copies, waits for them, and re-layouts  2.49 us (2%)
    pallas_call x1, Pallas kernels, per_device(): pl.pallas_call(functools.partial(kernel, ndev), out_shape=jax.ShapeDtypeS...  106 us
    unnamed x1, local copies, waits for them, and re-layouts  2.49 us

profile of v2, /device:TPU:0, one launch (start us, length us, event | category | flops | bytes accessed | tf_op | source)
XLA Modules:
  0.0 108.4 jit_solution(6533139064695705520)
XLA Ops:
  0.0 105.9 %shard_map.109 = bf16[1024,640]{1,0:T(8,128)(2,1)} custom-call(bf16[8,128,640]{2,1,0:T(8,128)(2,1)} %bitcast.3, bf16[128,640]{1,0:T(8,128)(2,1)} %own_ref.1, bf16[640,640]{1,0:T(8,128)(2,1)} %wq.1, bf16[640,640]{1,0:T(8,128)(2,1)} %wk.1, bf16[640,640]{1,0:T(8,128)(2,1)} %wv.1, bf16[640,640]{1,0:T(8,128)(2,1)} %wo.1, bf16[3,640,640]{2,1,0:T(8,128)(2,1)} %wc.1, ...), custom_call_target="tpu_custom_call" | custom-call | tf_op jit(solution)/shard_map/pallas_call | solution.py:291
  105.9 2.5 %copy.13 = bf16[1,1024,640]{2,1,0:T(8,128)(2,1)} copy(bf16[1,1024,640]{2,1,0:T(8,128)(2,1)} %bitcast.2) | data formatting | bytes 2621440

commit v3 on v2

--- a/solution.py
+++ b/solution.py
@@ -180,7 +180,7 @@
                 masked = jnp.where(low, queries, zero) if half == 0 else jnp.where(low, zero, queries)
                 scores = dot_nt(masked, keys)
                 peak = jnp.max(scores, axis=-1, keepdims=True)
-                expo = jnp.exp2(scores - peak).astype(BF16)
+                expo = jnp.exp2((scores - peak).astype(BF16))
                 both = dot(expo, values)
                 mixed.append(both[:, :128] / both[:, 128:])
             abuf[:, lanes] = jnp.where(low, mixed[0], mixed[1]).astype(BF16)

time: 109 us -> 109 us (level)
  no operation moved by 1% of the time
where the time goes in v3:
time: 109 us; the launch traced here: 108 us
  Pallas kernels  106 us (97%)
  local copies, waits for them, and re-layouts  2.49 us (2%)
    pallas_call x1, Pallas kernels, per_device(): pl.pallas_call(functools.partial(kernel, ndev), out_shape=jax.ShapeDtypeS...  106 us
    unnamed x1, local copies, waits for them, and re-layouts  2.49 us

profile of v3, /device:TPU:0, one launch (start us, length us, event | category | flops | bytes accessed | tf_op | source)
XLA Modules:
  0.0 108.5 jit_solution(13640525628440742799)
XLA Ops:
  0.0 106.0 %shard_map.109 = bf16[1024,640]{1,0:T(8,128)(2,1)} custom-call(bf16[8,128,640]{2,1,0:T(8,128)(2,1)} %bitcast.3, bf16[128,640]{1,0:T(8,128)(2,1)} %own_ref.1, bf16[640,640]{1,0:T(8,128)(2,1)} %wq.1, bf16[640,640]{1,0:T(8,128)(2,1)} %wk.1, bf16[640,640]{1,0:T(8,128)(2,1)} %wv.1, bf16[640,640]{1,0:T(8,128)(2,1)} %wo.1, bf16[3,640,640]{2,1,0:T(8,128)(2,1)} %wc.1, ...), custom_call_target="tpu_custom_call" | custom-call | tf_op jit(solution)/shard_map/pallas_call | solution.py:291
  106.0 2.5 %copy.13 = bf16[1,1024,640]{2,1,0:T(8,128)(2,1)} copy(bf16[1,1024,640]{2,1,0:T(8,128)(2,1)} %bitcast.2) | data formatting | bytes 2621440
